TPU v7x, 32 devices: a whole 2x2x4 slice. The times are simulated.
32 devices in a mesh: fsdp: 8 (over z, x), tp: 4 (over y, core).
Axes of the slice: x: 2, y: 2, z: 4, core: 2. Of those that a mesh axis runs over, the one named last changes fastest.
Arguments:
- tokens: bfloat16 [8, 2048, 768], P('fsdp', 'tp'), may hold values from -6 to 6
- lengths: int32 [8, 4], P('fsdp'), may hold values from 288 to 1024, as said below
- pictures: int32 [8, 2048], P('fsdp'), may hold values from 0 to 3, as said below
- w_query: bfloat16 [768, 768], P('fsdp', 'tp'), may hold values from -0.21875 to 0.21875
- w_key: bfloat16 [768, 768], P('fsdp', 'tp'), may hold values from -0.21875 to 0.21875
- w_value: bfloat16 [768, 768], P('fsdp', 'tp'), may hold values from -0.21875 to 0.21875
- w_out: bfloat16 [768, 768], P('tp', 'fsdp'), may hold values from -0.875 to 0.875
- w_up: bfloat16 [768, 3072], P('fsdp', 'tp'), may hold values from -0.21875 to 0.21875
- w_down: bfloat16 [3072, 768], P('tp', 'fsdp'), may hold values from -0.15625 to 0.15625
- norm1_gain: float32 [768], P(('fsdp', 'tp')), may hold values from 0.5 to 1.5
- norm1_shift: float32 [768], P(('fsdp', 'tp')), may hold values from -1.75 to 1.75
- norm2_gain: float32 [768], P(('fsdp', 'tp')), may hold values from 0.5 to 1.5
- norm2_shift: float32 [768], P(('fsdp', 'tp')), may hold values from -1.75 to 1.75
- query_gain: float32 [768], P(('fsdp', 'tp')), may hold values from 1 to 2
- key_gain: float32 [768], P(('fsdp', 'tp')), may hold values from 1 to 2
- cotangent: bfloat16 [8, 2048, 768], P('fsdp', 'tp'), may hold values from -6 to 6
Outputs:
- layer_out: bfloat16 [8, 2048, 768], P('fsdp', 'tp')
- input_grad: float32 [8, 2048, 768], P('fsdp', 'tp')
- grad_query: float32 [768, 768], P('fsdp', 'tp')
- grad_key: float32 [768, 768], P('fsdp', 'tp')
- grad_value: float32 [768, 768], P('fsdp', 'tp')
- grad_output_proj: float32 [768, 768], P('tp', 'fsdp')
- grad_up: float32 [768, 3072], P('fsdp', 'tp')
- grad_down: float32 [3072, 768], P('tp', 'fsdp')
- grad_norm1_gain: float32 [768], P(('fsdp', 'tp'))
- grad_norm1_shift: float32 [768], P(('fsdp', 'tp'))
- grad_norm2_gain: float32 [768], P(('fsdp', 'tp'))
- grad_norm2_shift: float32 [768], P(('fsdp', 'tp'))
- grad_query_gain: float32 [768], P(('fsdp', 'tp'))
- grad_key_gain: float32 [768], P(('fsdp', 'tp'))
- statistics: float32 [4], replicated
Inputs may be any that keep to these rules, and one draw needn't show every extreme that they name: The lengths of a row sum to at most 2048; one picture of every row has exactly 1024 patches. Slots of a row carry the pictures in order, each picture covering as many slots as its length; slots after the row's total length repeat the last picture's number.
All inputs are finite; a program needn't handle non-finite values.
Results may differ from a plain program's by a relative error of at most 0.018.
Values may be sent and summed in bfloat16 or wider, within the bound.
A program may use at most 192 MiB of HBM per device.

v0:
```python
import functools

import jax
import jax.numpy as jnp
from jax import lax
from jax.experimental import pallas as pl
from jax.experimental.pallas import tpu as pltpu
from jax.sharding import PartitionSpec as P

HD = 64


EPS = 1e-06
ROOT_HALF = 0.7071067811865476
DENSITY = 0.3989422804014327


def normalise(values, scaling, offset):
    centre = jnp.mean(values, axis=-1, keepdims=True)
    centred = values - centre
    spread = jnp.mean(centred * centred, axis=-1, keepdims=True)
    inverse = lax.rsqrt(spread + EPS)
    normed = centred * inverse
    return (normed * scaling + offset, normed, inverse)


def normalise_back(grad_out, normed, inverse, scaling):
    grad_unit = grad_out * scaling
    grad_values = inverse * (
        grad_unit
        - jnp.mean(grad_unit, axis=-1, keepdims=True)
        - normed * jnp.mean(grad_unit * normed, axis=-1, keepdims=True)
    )
    return (grad_values, jnp.sum(grad_out * normed, axis=(0, 1)), jnp.sum(grad_out, axis=(0, 1)))


def gelu_slope(values):
    return (
        0.5 * (1.0 + jax.scipy.special.erf(values * ROOT_HALF))
        + values * jnp.exp(-0.5 * values * values) * DENSITY
    )


def gather_tokens(values):
    return lax.all_gather(values, "tp", axis=1, tiled=True)


def gather_grads(values):
    return lax.all_gather(values, "tp", axis=1, tiled=True)


def reduce_tokens(values):
    return lax.psum_scatter(
        values.astype(jnp.bfloat16), "tp", scatter_dimension=1, tiled=True
    ).astype(jnp.float32)


def reduce_grads(values):
    return lax.psum_scatter(
        values.astype(jnp.bfloat16), "tp", scatter_dimension=1, tiled=True
    ).astype(jnp.float32)


def block_scores(query, keyed, picture_query, picture_key, key_mask):
    raw_scores = jnp.einsum("qhd,khd->hqk", query, keyed, preferred_element_type=jnp.float32)
    allowed = (picture_query[:, None] == picture_key[None, :]) & (key_mask[None, :] > 0)
    return jnp.where(allowed[None], raw_scores * query.shape[-1] ** (-0.5), -1e30)


def forward_row(packed):
    query_row, key_row, value_row, picture_row, mask_row = packed
    full_len = query_row.shape[0]
    block_len = min(512, full_len)
    block_count = full_len // block_len

    def forward_one_block(packed_block):
        query_block, picture_block = packed_block
        scores = block_scores(query_block, key_row, picture_block, picture_row, mask_row)
        highest = jnp.max(scores, axis=-1, keepdims=True)
        logsum = highest + jnp.log(jnp.sum(jnp.exp(scores - highest), axis=-1, keepdims=True))
        probability = jnp.exp(scores - logsum).astype(jnp.bfloat16)
        mixture = jnp.einsum(
            "hqk,khd->qhd", probability, value_row, preferred_element_type=jnp.float32
        )
        return (mixture, logsum)

    query_blocks = query_row.reshape((block_count, block_len) + query_row.shape[1:])
    return lax.map(forward_one_block, (query_blocks, picture_row.reshape(block_count, block_len)))


def backward_row(packed):
    query_row, key_row, value_row, picture_row, mask_row, grad_row, logsum_row = packed
    full_len = query_row.shape[0]
    block_len = min(512, full_len)
    block_count = full_len // block_len
    factor = query_row.shape[-1] ** (-0.5)

    def backward_one_block(running, packed_block):
        grad_key, grad_value = running
        query_block, picture_block, grad_block, logsum_block = packed_block
        scores = block_scores(query_block, key_row, picture_block, picture_row, mask_row)
        probability = jnp.exp(scores - logsum_block)
        prob_low = probability.astype(jnp.bfloat16)
        grad_prob = jnp.einsum(
            "qhd,khd->hqk", grad_block, value_row, preferred_element_type=jnp.float32
        )
        grad_value = grad_value + jnp.einsum(
            "hqk,qhd->khd", prob_low, grad_block, preferred_element_type=jnp.float32
        )
        centre = jnp.sum(probability * grad_prob, axis=-1, keepdims=True)
        grad_scores = (probability * (grad_prob - centre)).astype(jnp.bfloat16)
        grad_query = factor * jnp.einsum(
            "hqk,khd->qhd", grad_scores, key_row, preferred_element_type=jnp.float32
        )
        grad_key = grad_key + factor * jnp.einsum(
            "hqk,qhd->khd", grad_scores, query_block, preferred_element_type=jnp.float32
        )
        return ((grad_key, grad_value), grad_query)

    zero_state = jnp.zeros(key_row.shape, jnp.float32)
    block_shape = (block_count, block_len) + query_row.shape[1:]
    (grad_key, grad_value), grad_query = lax.scan(
        backward_one_block,
        (zero_state, zero_state),
        (
            query_row.reshape(block_shape),
            picture_row.reshape(block_count, block_len),
            grad_row.reshape(block_shape),
            logsum_row,
        ),
    )
    return (grad_query.reshape(key_row.shape), grad_key, grad_value)


def local_plain(
    tokens,
    lengths,
    pictures,
    w_query,
    w_key,
    w_value,
    w_out,
    w_up,
    w_down,
    norm1_gain,
    norm1_shift,
    norm2_gain,
    norm2_shift,
    query_gain,
    key_gain,
    cotangent,
):
    tp_place = lax.axis_index("tp")
    local_len = tokens.shape[1]
    model_width = tokens.shape[2]
    full_len = pictures.shape[1]
    local_width = w_query.shape[1]
    heads_local = local_width // HD
    gain_one, shift_one, gain_two, shift_two, gain_query, gain_key = (
        lax.all_gather(norm1_gain, ("fsdp", "tp"), axis=0, tiled=True),
        lax.all_gather(norm1_shift, ("fsdp", "tp"), axis=0, tiled=True),
        lax.all_gather(norm2_gain, ("fsdp", "tp"), axis=0, tiled=True),
        lax.all_gather(norm2_shift, ("fsdp", "tp"), axis=0, tiled=True),
        lax.all_gather(query_gain, ("fsdp", "tp"), axis=0, tiled=True),
        lax.all_gather(key_gain, ("fsdp", "tp"), axis=0, tiled=True),
    )
    positions = jnp.arange(full_len, dtype=jnp.int32)
    valid_full = (positions[None, :] < jnp.sum(lengths, axis=1)[:, None]).astype(jnp.float32)
    valid_here = lax.dynamic_slice_in_dim(valid_full, tp_place * local_len, local_len, 1)[
        :, :, None
    ]
    qgain_here = lax.dynamic_slice_in_dim(
        gain_query, tp_place * local_width, local_width, 0
    ).reshape(heads_local, HD)
    kgain_here = lax.dynamic_slice_in_dim(gain_key, tp_place * local_width, local_width, 0).reshape(
        heads_local, HD
    )
    front_query, front_key, front_value, front_out = (
        lax.all_gather(w_query, "fsdp", axis=0, tiled=True),
        lax.all_gather(w_key, "fsdp", axis=0, tiled=True),
        lax.all_gather(w_value, "fsdp", axis=0, tiled=True),
        lax.all_gather(w_out, "fsdp", axis=1, tiled=True),
    )
    inputs = tokens.astype(jnp.float32)
    hidden, normed_one, inverse_one = normalise(inputs, gain_one, shift_one)
    hidden_full = gather_tokens(hidden.astype(jnp.bfloat16))
    row_shape = hidden_full.shape[:2] + (heads_local, HD)
    query = jnp.dot(hidden_full, front_query, preferred_element_type=jnp.float32).reshape(row_shape)
    keyed = jnp.dot(hidden_full, front_key, preferred_element_type=jnp.float32).reshape(row_shape)
    value_low = (
        jnp.dot(hidden_full, front_value, preferred_element_type=jnp.float32)
        .astype(jnp.bfloat16)
        .reshape(row_shape)
    )
    query_norm, query_unit, query_inverse = normalise(query, qgain_here, 0.0)
    key_norm, key_unit, key_inverse = normalise(keyed, kgain_here, 0.0)
    query_low = query_norm.astype(jnp.bfloat16)
    key_low = key_norm.astype(jnp.bfloat16)
    mixture, logsum = lax.map(forward_row, (query_low, key_low, value_low, pictures, valid_full))
    mixture_low = mixture.reshape(hidden_full.shape[:2] + (local_width,)).astype(jnp.bfloat16)
    attn_branch = valid_here * reduce_tokens(
        jnp.dot(mixture_low, front_out, preferred_element_type=jnp.float32)
    )
    middle = inputs + attn_branch
    hidden_two, normed_two, inverse_two = normalise(middle, gain_two, shift_two)
    hidden_two_full = gather_tokens(hidden_two.astype(jnp.bfloat16))
    front_up, front_down = (
        lax.all_gather(w_up, "fsdp", axis=0, tiled=True),
        lax.all_gather(w_down, "fsdp", axis=1, tiled=True),
    )
    up_value = jnp.dot(hidden_two_full, front_up, preferred_element_type=jnp.float32)
    activated = jax.nn.gelu(up_value, approximate=False).astype(jnp.bfloat16)
    mlp_branch = valid_here * reduce_tokens(
        jnp.dot(activated, front_down, preferred_element_type=jnp.float32)
    )
    result = (middle + mlp_branch).astype(jnp.bfloat16)
    square_sums = jnp.stack(
        [
            jnp.sum(valid_here * inputs * inputs),
            jnp.sum(attn_branch * attn_branch),
            jnp.sum(valid_here * middle * middle),
            jnp.sum(mlp_branch * mlp_branch),
        ]
    )
    valid_count = jnp.sum(valid_here)
    back_up, back_down = (
        lax.all_gather(w_up, "fsdp", axis=0, tiled=True),
        lax.all_gather(w_down, "fsdp", axis=1, tiled=True),
    )
    back_query, back_key, back_value, back_out = (
        lax.all_gather(w_query, "fsdp", axis=0, tiled=True),
        lax.all_gather(w_key, "fsdp", axis=0, tiled=True),
        lax.all_gather(w_value, "fsdp", axis=0, tiled=True),
        lax.all_gather(w_out, "fsdp", axis=1, tiled=True),
    )
    grad_y = cotangent.astype(jnp.float32) * valid_here
    grad_y_full = gather_grads(grad_y.astype(jnp.bfloat16))
    grad_down = jnp.einsum(
        "rlf,rld->fd", activated, grad_y_full, preferred_element_type=jnp.float32
    )
    grad_act = jnp.dot(grad_y_full, back_down.T, preferred_element_type=jnp.float32)
    grad_pre = (grad_act * gelu_slope(up_value)).astype(jnp.bfloat16)
    grad_up = jnp.einsum(
        "rld,rlf->df", hidden_two_full, grad_pre, preferred_element_type=jnp.float32
    )
    grad_hidden_two = reduce_grads(jnp.dot(grad_pre, back_up.T, preferred_element_type=jnp.float32))
    mlp_grads = (
        lax.psum_scatter(grad_up, "fsdp", scatter_dimension=0, tiled=True),
        lax.psum_scatter(grad_down, "fsdp", scatter_dimension=1, tiled=True),
    )
    grad_mid_norm, grad_gain_two, grad_shift_two = normalise_back(
        grad_hidden_two, normed_two, inverse_two, gain_two
    )
    grad_middle = grad_y + grad_mid_norm
    grad_branch_here = (valid_here * grad_middle).astype(jnp.bfloat16)
    grad_branch_full = gather_grads(grad_branch_here)
    grad_out_proj = jnp.einsum(
        "rlh,rld->hd", mixture_low, grad_branch_full, preferred_element_type=jnp.float32
    )
    grad_mixture = jnp.dot(grad_branch_full, back_out.T, preferred_element_type=jnp.float32).astype(
        jnp.bfloat16
    )
    grad_qnorm, grad_knorm, grad_value_full = lax.map(
        backward_row,
        (
            query_low,
            key_low,
            value_low,
            pictures,
            valid_full,
            grad_mixture.reshape(row_shape),
            logsum,
        ),
    )
    grad_query_pre, grad_qgain, unused_one = normalise_back(
        grad_qnorm, query_unit, query_inverse, qgain_here
    )
    grad_key_pre, grad_kgain, unused_two = normalise_back(
        grad_knorm, key_unit, key_inverse, kgain_here
    )
    flat_shape = hidden_full.shape[:2] + (local_width,)
    grad_query_low = grad_query_pre.reshape(flat_shape).astype(jnp.bfloat16)
    grad_key_low = grad_key_pre.reshape(flat_shape).astype(jnp.bfloat16)
    grad_value_low = grad_value_full.reshape(flat_shape).astype(jnp.bfloat16)
    grad_wquery = jnp.einsum(
        "rld,rlh->dh", hidden_full, grad_query_low, preferred_element_type=jnp.float32
    )
    grad_wkey = jnp.einsum(
        "rld,rlh->dh", hidden_full, grad_key_low, preferred_element_type=jnp.float32
    )
    grad_wvalue = jnp.einsum(
        "rld,rlh->dh", hidden_full, grad_value_low, preferred_element_type=jnp.float32
    )
    grad_hidden_part = (
        jnp.dot(grad_query_low, back_query.T, preferred_element_type=jnp.float32)
        + jnp.dot(grad_key_low, back_key.T, preferred_element_type=jnp.float32)
        + jnp.dot(grad_value_low, back_value.T, preferred_element_type=jnp.float32)
    )
    grad_hidden = reduce_grads(grad_hidden_part)
    attn_grads = (
        lax.psum_scatter(grad_wquery, "fsdp", scatter_dimension=0, tiled=True),
        lax.psum_scatter(grad_wkey, "fsdp", scatter_dimension=0, tiled=True),
        lax.psum_scatter(grad_wvalue, "fsdp", scatter_dimension=0, tiled=True),
        lax.psum_scatter(grad_out_proj, "fsdp", scatter_dimension=1, tiled=True),
    )
    grad_in_norm, grad_gain_one, grad_shift_one = normalise_back(
        grad_hidden, normed_one, inverse_one, gain_one
    )
    grad_inputs = grad_middle + grad_in_norm
    zero_width = jnp.zeros((model_width,), jnp.float32)
    grad_qgain_full = lax.dynamic_update_slice_in_dim(
        zero_width, grad_qgain.reshape(local_width), tp_place * local_width, 0
    )
    grad_kgain_full = lax.dynamic_update_slice_in_dim(
        zero_width, grad_kgain.reshape(local_width), tp_place * local_width, 0
    )
    small_shards = (
        lax.psum_scatter(grad_gain_one, ("fsdp", "tp"), scatter_dimension=0, tiled=True),
        lax.psum_scatter(grad_shift_one, ("fsdp", "tp"), scatter_dimension=0, tiled=True),
        lax.psum_scatter(grad_gain_two, ("fsdp", "tp"), scatter_dimension=0, tiled=True),
        lax.psum_scatter(grad_shift_two, ("fsdp", "tp"), scatter_dimension=0, tiled=True),
        lax.psum_scatter(grad_qgain_full, ("fsdp", "tp"), scatter_dimension=0, tiled=True),
        lax.psum_scatter(grad_kgain_full, ("fsdp", "tp"), scatter_dimension=0, tiled=True),
    )
    totals, counted = lax.psum((square_sums, valid_count), ("fsdp", "tp"))
    statistics = jnp.sqrt(totals / (counted * model_width))
    return (
        result,
        grad_inputs,
        attn_grads[0],
        attn_grads[1],
        attn_grads[2],
        attn_grads[3],
        mlp_grads[0],
        mlp_grads[1],
        small_shards[0],
        small_shards[1],
        small_shards[2],
        small_shards[3],
        small_shards[4],
        small_shards[5],
        statistics,
    )


BIG = 1024
SMALL = 448
LP = BIG + 3 * SMALL
MARGIN = 128
EXP_SCALE = 0.125 * 1.4426950408889634
MESH = pl.DeviceIdType.MESH
BF = jnp.bfloat16
F32 = jnp.float32


def dot_nn(a, b):
    return lax.dot_general(a, b, (((1,), (0,)), ((), ())), preferred_element_type=F32)


def dot_nt(a, b):
    return lax.dot_general(a, b, (((1,), (1,)), ((), ())), preferred_element_type=F32)


def dot_tn(a, b):
    return lax.dot_general(a, b, (((0,), (0,)), ((), ())), preferred_element_type=F32)


def iota(shape, dim):
    return lax.broadcasted_iota(jnp.int32, shape, dim)


def head_mask(rows, width, h):
    lane = iota((rows, width), 1)
    return (lane >= h * HD) & (lane < (h + 1) * HD)


def segment_matrix(width):
    r = iota((width, width), 0) // HD
    c = iota((width, width), 1) // HD
    return jnp.where(r == c, 1.0 / HD, 0.0).astype(BF)


def segment_mean(x, seg):
    return dot_nn(x.astype(BF), seg)


class Place:
    def __init__(self, nf, nt):
        self.nf, self.nt = nf, nt
        self.nx = 2
        self.nz = nf // 2
        f = lax.axis_index("fsdp")
        t = lax.axis_index("tp")
        self.f, self.t = f, t
        self.z, self.x = f // 2, lax.rem(f, 2)
        self.y, self.c = t // 2, lax.rem(t, 2)
        self.me = f * nt + t

    def rel(self, dz=0, dx=0, dy=0, dc=0):
        z = lax.rem(self.z + dz, self.nz) if dz else self.z
        x = 1 - self.x if dx else self.x
        y = 1 - self.y if dy else self.y
        c = 1 - self.c if dc else self.c
        return (z * 2 + x, y * 2 + c)


class Copies:
    def __init__(self):
        self.sent = []

    def start(self, src, dst, send_sem, recv_sem, dev):
        cp = pltpu.make_async_remote_copy(
            src_ref=src,
            dst_ref=dst,
            send_sem=send_sem,
            recv_sem=recv_sem,
            device_id=dev,
            device_id_type=MESH,
        )
        cp.start()
        self.sent.append(cp)

    def finish(self):
        for cp in self.sent:
            cp.wait_send()
        self.sent = []


def wait_recv(dst, send_sem, recv_sem, dev):
    pltpu.make_async_remote_copy(
        src_ref=dst,
        dst_ref=dst,
        send_sem=send_sem,
        recv_sem=recv_sem,
        device_id=dev,
        device_id_type=MESH,
    ).wait_recv()


def barrier_peers(pc):
    steps = [dict(dz=i) for i in range(1, pc.nz)]
    steps += [dict(dx=1), dict(dy=1), dict(dc=1), dict(dy=1, dc=1)]
    bar = pltpu.get_barrier_semaphore()
    for step in steps:
        pl.semaphore_signal(bar, inc=1, device_id=pc.rel(**step), device_id_type=MESH)
    pl.semaphore_wait(bar, len(steps))


def axis_steps(pc, axis):
    if axis == "z":
        return [dict(dz=i) for i in range(1, pc.nz)]
    return [{"d" + axis: 1}]


def sends_of(nz, order):
    return sum(nz - 1 if axis == "z" else 1 for axis in order)


class Gather:
    def __init__(self, pc, copies, src, dst, send, recv, dims, order):
        self.pc, self.copies = pc, copies
        self.src, self.dst, self.send_sem, self.recv_sem = src, dst, send, recv
        self.dims, self.order = dims, order
        self.stages = []
        count = 0
        for axis in order:
            steps = axis_steps(pc, axis)
            self.stages.append([(count + i, step) for i, step in enumerate(steps)])
            count += len(steps)

    def index(self, stage, at=None):
        place = at or dict(z=self.pc.z, x=self.pc.x, y=self.pc.y, c=self.pc.c)
        done = self.order[:stage]
        return tuple(slice(None) if d in done else place[d] for d in self.dims)

    def keep(self, sem):
        self.local = pltpu.make_async_copy(self.src, self.dst.at[self.index(0)], sem)
        self.local.start()

    def send(self, k):
        if k == 1:
            self.local.wait()
        idx = self.index(k)
        src = self.src if k == 0 else self.dst.at[idx]
        for n, step in self.stages[k]:
            self.copies.start(
                src, self.dst.at[idx], self.send_sem.at[n], self.recv_sem.at[n], self.pc.rel(**step)
            )

    def wait(self, k):
        pc = self.pc
        for n, step in self.stages[k]:
            at = dict(z=pc.z, x=pc.x, y=pc.y, c=pc.c)
            if "dz" in step:
                at["z"] = lax.rem(pc.z + pc.nz - step["dz"], pc.nz)
            else:
                axis = self.order[k]
                at[axis] = 1 - at[axis]
            dst = self.dst.at[self.index(k, at)]
            wait_recv(dst, self.send_sem.at[n], self.recv_sem.at[n], pc.rel(**step))


def slots_of(lens_ref):
    lens = [lens_ref[0, p] for p in range(4)]
    starts = [0]
    for p in range(3):
        starts.append(starts[-1] + lens[p])
    big = 0
    for p in range(1, 4):
        big = jnp.where(lens[p] == BIG, p, big)
    sb = 0
    for p in range(1, 4):
        sb = jnp.where(big == p, starts[p], sb)
    out = [(sb, BIG)]
    for k in range(3):
        s = jnp.where(big <= k, starts[k + 1], starts[k])
        n = jnp.where(big <= k, lens[k + 1], lens[k])
        out.append((s, n))
    return out


def small_length(lens, k):
    slots = slots_of(lens)
    return jnp.where(k == 0, slots[1][1], jnp.where(k == 1, slots[2][1], slots[3][1]))


BASES = (0, BIG, BIG + SMALL, BIG + 2 * SMALL)


def shift_matrix(rows, cols, r):
    return jnp.where(iota((rows, cols), 1) == iota((rows, cols), 0) + r, 1.0, 0.0).astype(BF)


def load_rows(src, first, count):
    return jnp.concatenate([src[first + m] for m in range(count)], axis=0)


def pack_rows(src, dst, lens, masked=False):
    def big(j, carry):
        s = slots_of(lens)[0][0]
        r = lax.rem(s, 16)
        d = shift_matrix(128, 144, r)
        out = dot_nn(d, load_rows(src, s // 16 + j * 8, 9)).astype(BF)
        dst[pl.ds(pl.multiple_of(j * 128, 128), 128), :] = out
        return carry

    lax.fori_loop(0, BIG // 128, big, 0)

    for k in range(3):

        def small(j, carry, k=k):
            s, n = slots_of(lens)[1 + k]
            r = lax.rem(s, 16)
            d = shift_matrix(112, 128, r)
            out = dot_nn(d, load_rows(src, s // 16 + j * 7, 8))
            if masked:
                out = jnp.where(iota(out.shape, 0) + j * 112 < n, out, 0.0)
            out = out.astype(BF)
            dst[pl.ds(pl.multiple_of(BASES[1 + k] + j * 112, 16), 112), :] = out
            return carry

        lax.fori_loop(0, 4, small, 0)


def unpack_tile(src, i0, lens):
    wa, ea, wb, sb = 0, 0, 0, 4096
    for (s, n), base in zip(slots_of(lens), BASES):
        inside = (s <= i0) & (i0 < s + n)
        begins = (s > i0) & (s <= i0 + 127)
        w = base + i0 - s + MARGIN
        wa = jnp.where(inside, w, wa)
        ea = jnp.where(inside, s + n - i0, ea)
        wb = jnp.where(begins, w, wb)
        sb = jnp.where(begins, s - i0, sb)
    out = None
    row = iota((128, 144), 0)
    col = iota((128, 144), 1)
    for w, ok in ((wa, lambda: row < ea), (wb, lambda: row >= sb)):
        r = lax.rem(w, 16)
        d = jnp.where((col == row + r) & ok(), 1.0, 0.0).astype(BF)
        part = dot_nn(d, load_rows(src, w // 16, 9))
        out = part if out is None else out + part
    return out


def layer_norm_rows(x, g, b):
    mean = jnp.mean(x, axis=-1, keepdims=True)
    xc = x - mean
    var = jnp.mean(xc * xc, axis=-1, keepdims=True)
    inv = lax.rsqrt(var + EPS)
    n = xc * inv
    return n * g + b, n, inv


def own_heads(row, t, nt, width):
    out = row[:, :width]
    for k in range(1, nt):
        out = jnp.where(t == k, row[:, k * width : (k + 1) * width], out)
    return out


def build_gains(tiles, gains, per):
    chunks = len(tiles) * per // 128
    lane = iota((8, 128), 1)
    acc = [jnp.zeros((8, 128), F32) for _ in range(chunks)]
    for d, tile in enumerate(tiles):
        j, a = divmod(d * per, 128)
        if a:
            tile = pltpu.roll(tile, a, 1)
        acc[j] = jnp.where((lane >= a) & (lane < a + per), tile, acc[j])
        if a + per > 128:
            acc[j + 1] = jnp.where(lane < a + per - 128, tile, acc[j + 1])
    for j in range(chunks):
        gains[:, j * 128 : (j + 1) * 128] = acc[j]


def ka_kernel(
    nf, nt, orders,
    lens, tok, wq, wk, wv, wo_in, wu, wd, s0, s1, s2, s3, s4, s5,
    qkv_out, lse_out, ob_out, wqkv, gains, o_own, h1_out, wo_all, wu0_all, wu1_all, wd0_all, wd1_all,
    wa, wo, prm, qkv, lse, ob, tok_all, h1t, h1p, wa_all, prm_all, of, op, osend,
    prm_s, prm_r, tok_s, tok_r, wa_s, wa_r, wo_s, wo_r,
    u0_s, u0_r, u1_s, u1_r, d0_s, d0_r, d1_s, d1_r, o_s, o_r, loc,
):
    pc = Place(nf, nt)
    cps = Copies()
    rows, width = tok.shape
    hw = ob.shape[1]
    cut = width // 2
    wa[...] = jnp.concatenate([wq[...], wk[...], wv[...]], axis=1)
    wo[...] = wo_in[...].T
    prm[...] = jnp.zeros(prm.shape, F32)
    for i, small in enumerate((s0, s1, s2, s3, s4, s5)):
        prm[i : i + 1, : small.shape[1]] = small[...]
    gp = Gather(pc, cps, prm, prm_all, prm_s, prm_r, "zxyc", orders["prm"])
    ga = Gather(pc, cps, wa, wa_all, wa_s, wa_r, "zx", orders["wa"])
    go = Gather(pc, cps, wo, wo_all, wo_s, wo_r, "yczx", orders["wo"])
    gu0 = Gather(pc, cps, wu.at[:, :cut], wu0_all, u0_s, u0_r, "yzx", orders["u0"])
    gu1 = Gather(pc, cps, wu.at[:, cut:], wu1_all, u1_s, u1_r, "yzx", orders["u1"])
    gd0 = Gather(pc, cps, wd.at[:, :cut], wd0_all, d0_s, d0_r, "yzx", orders["d0"])
    gd1 = Gather(pc, cps, wd.at[:, cut:], wd1_all, d1_s, d1_r, "yzx", orders["d1"])
    for i, g in enumerate((gp, ga, go, gd1, gu0, gd0, gu1)):
        g.keep(loc.at[i])
    barrier_peers(pc)

    cps.start(tok, tok_all.at[pc.t], tok_s.at[1], tok_r.at[pc.t], pc.rel(dc=1))
    gp.send(0)
    ga.send(0)
    gd1.send(0)
    cps.start(tok, tok_all.at[pc.t], tok_s.at[0], tok_r.at[pc.t], pc.rel(dy=1))
    h1t[4 * rows // 16 :] = jnp.zeros((h1t.shape[0] - 4 * rows // 16, 16, width), BF)
    for k in range(4):
        gp.wait(k)
        if k < 3:
            gp.send(k + 1)
    gd1.wait(0)
    gd1.send(1)
    go.send(0)
    tiles = []
    for d in range(nf * nt):
        f, t = divmod(d, nt)
        tiles.append(prm_all[f // 2, f % 2, t // 2, t % 2])
    build_gains(tiles, gains, width // (nf * nt))
    gain_one, shift_one = gains[0:1, :], gains[1:2, :]

    def norm_block(t, block):
        def body(j, carry):
            at = pl.ds(pl.multiple_of(j * 128, 128), 128)
            out, _, _ = layer_norm_rows(block[at, :].astype(F32), gain_one, shift_one)
            h1t[pl.ds(t * (rows // 16) + j * 8, 8)] = out.astype(BF).reshape(8, 16, width)
            return carry

        lax.fori_loop(0, rows // 128, body, 0)

    def wait_tok(t):
        wait_recv(tok_all.at[t], tok_s.at[0], tok_r.at[t], pc.rel(dc=1))

    norm_block(pc.t, tok)
    t_core, t_y, t_diag = pc.rel(dc=1)[1], pc.rel(dy=1)[1], pc.rel(dy=1, dc=1)[1]
    wait_tok(t_core)
    norm_block(t_core, tok_all.at[t_core])
    ga.wait(0)
    ga.send(1)
    gu0.send(0)
    gd0.send(0)
    wait_tok(t_y)
    cps.start(tok_all.at[t_y], tok_all.at[t_y], tok_s.at[2], tok_r.at[t_y], pc.rel(dc=1))
    norm_block(t_y, tok_all.at[t_y])
    wait_tok(t_diag)
    norm_block(t_diag, tok_all.at[t_diag])
    h1_copy = pltpu.make_async_copy(h1t.at[: 4 * rows // 16], h1_out, loc.at[0])
    h1_copy.start()

    pack_rows(h1t, h1p, lens)
    go.wait(0)
    go.send(1)
    gu0.wait(0)
    gu0.send(1)
    gd0.wait(0)
    gd0.send(1)
    gu1.send(0)
    gd1.wait(1)
    ga.wait(1)
    seg = segment_matrix(hw)
    gq = own_heads(gains[4:5, :], pc.t, nt, hw)
    gk = own_heads(gains[5:6, :], pc.t, nt, hw)
    w_full = wa_all[...].reshape(width, 3 * hw)
    for i in range(3):
        wqkv[i] = w_full[:, i * hw : (i + 1) * hw]

    qt = LP // 4

    def project(j, carry):
        at = pl.ds(pl.multiple_of(j * qt, 16), qt)
        h = h1p[at, :]
        lane = iota((qt, 128), 1)
        kept = jnp.zeros((qt, 128), F32)
        for i, g in enumerate((gq, gk)):
            q = dot_nn(h, wqkv[i])
            qc = q - segment_mean(q, seg)
            inv = lax.rsqrt(segment_mean(qc * qc, seg) + EPS)
            qkv[at, i * 256 : i * 256 + hw] = (qc * inv * g).astype(BF)
            for k in range(hw // HD):
                kept = jnp.where(lane == 8 * (i + 1) + k, inv[:, k * HD : k * HD + 1], kept)
        lse[at, :] = kept
        qkv[at, 512 : 512 + hw] = dot_nn(h, wqkv[2]).astype(BF)
        return carry

    lax.fori_loop(0, 4, project, 0)
    qkv[:, 512 + hw :] = jnp.ones((LP, 256 - hw), BF)
    saves = [h1_copy, pltpu.make_async_copy(qkv, qkv_out, loc.at[2])]
    saves[-1].start()
    head, tail = MARGIN // 16, (MARGIN + LP) // 16
    op[:head] = jnp.zeros((head, 16, hw), BF)
    op[tail:] = jnp.zeros((op.shape[0] - tail, 16, hw), BF)

    gu0.wait(1)
    gu0.send(2)
    gu1.wait(0)
    gu1.send(1)
    gd0.wait(1)
    gd0.send(2)
    go.wait(1)
    go.send(2)
    gd1.send(2)

    def attend(at, keys, h, limit):
        nrow = at.size
        q = jnp.where(head_mask(nrow, hw, h), qkv[at, :hw], jnp.zeros((), BF))
        s = dot_nt(q, qkv[keys, 256 : 256 + hw])
        p = jnp.exp2(s * EXP_SCALE)
        if limit is not None:
            p = jnp.where(iota(p.shape, 1) < limit, p, 0.0)
        oa = dot_nn(p.astype(BF), qkv[keys, 512:768])
        total = oa[:, hw : hw + 1]
        o = oa[:, :hw] * (1.0 / total)
        l2 = jnp.log2(total)
        lane = iota((nrow, 128), 1)
        if h == 0:
            of[at, :] = o
        else:
            of[at, :] = jnp.where(head_mask(nrow, hw, h), o, of[at, :])
        lse[at, :] = jnp.where(lane == h, l2, lse[at, :])

    nh = hw // HD
    for h in range(nh):
        def big(j, carry, h=h):
            attend(pl.ds(pl.multiple_of(j * 512, 512), 512), pl.ds(0, BIG), h, None)
            return carry

        lax.fori_loop(0, BIG // 512, big, 0)

        def small(k, carry, h=h):
            at = pl.ds(pl.multiple_of(BIG + k * SMALL, 16), SMALL)
            attend(at, at, h, small_length(lens, k))
            return carry

        lax.fori_loop(0, 3, small, 0)
        if h == 1:
            gu1.wait(1)
            gu1.send(2)
        elif h == 2:
            go.wait(2)
            go.send(3)

    ob[...] = of[...].astype(BF)
    for i, (src, dst) in enumerate(((lse, lse_out), (ob, ob_out))):
        saves.append(pltpu.make_async_copy(src, dst, loc.at[3 + i]))
        saves[-1].start()
    op[head:tail] = ob[...].reshape(LP // 16, 16, hw)

    def unpack_block(t):
        def unpack(i, carry):
            out = unpack_tile(op, t * rows + i * 128, lens)
            osend[t, pl.ds(pl.multiple_of(i * 128, 128), 128), :] = out.astype(BF)
            return carry

        lax.fori_loop(0, rows // 128, unpack, 0)

    peers = [pc.rel(dy=1, dc=1), pc.rel(dy=1), pc.rel(dc=1)]
    for i, dev in enumerate(peers):
        unpack_block(dev[1])
        cps.start(osend.at[dev[1]], o_own.at[pc.t], o_s.at[i], o_r.at[pc.t], dev)
    unpack_block(pc.t)
    cp = pltpu.make_async_copy(osend.at[pc.t], o_own.at[pc.t], loc.at[1])
    cp.start()
    cp.wait()
    for cp in saves:
        cp.wait()
    go.wait(3)
    for g in (gu0, gd0, gu1, gd1):
        g.wait(2)
    for dev in peers:
        wait_recv(o_own.at[dev[1]], o_s.at[0], o_r.at[dev[1]], dev)
    cps.finish()


def call_ka(nf, nt, lens, tok, wq, wk, wv, wo, wu, wd, smalls):
    nz = nf // 2
    rows, width = tok.shape
    r, hw = wq.shape
    cut = width // 2
    orders = dict(
        prm=("z", "x", "y", "c"), wa=("z", "x"), wo=("z", "y", "x", "c"),
        u0=("z", "y", "x"), d0=("z", "x", "y"), u1=("z", "y", "x"), d1=("y", "x", "z"),
    )
    S = jax.ShapeDtypeStruct
    V = pltpu.VMEM
    vm = pl.BlockSpec(memory_space=pltpu.VMEM)
    hb = pl.BlockSpec(memory_space=pl.ANY)
    half = (S((2, nz, 2, r, cut), BF), hb)
    outs = [
        (S((LP, 768), BF), hb), (S((LP, 128), F32), hb), (S((LP, hw), BF), hb), (S((3, width, hw), BF), vm),
        (S((8, width), F32), vm), (S((nt, rows, hw), BF), vm),
        (S((nt * rows // 16, 16, width), BF), hb), (S((2, 2, nz, 2, r, hw), BF), hb), half, half, half, half,
    ]
    dma = pltpu.SemaphoreType.DMA
    scratch = [
        V((r, 3 * hw), BF), V((r, hw), BF), V((8, 128), F32),
        V((LP, 768), BF), V((LP, 128), F32), V((LP, hw), BF),
        V((nt, rows, width), BF), V(((nt * rows + 192) // 16, 16, width), BF), V((LP, width), BF),
        V((nz, 2, r, 3 * hw), BF), V((nz, 2, 2, 2, 8, 128), F32),
        V((LP, hw), F32), V(((MARGIN + LP + 160) // 16, 16, hw), BF), V((nt, rows, hw), BF),
    ]
    p = sends_of(nz, orders["prm"])
    scratch += [dma((p,)), dma((p,)), dma((3,)), dma((nt,))]
    for name in ("wa", "wo", "u0", "u1", "d0", "d1"):
        p = sends_of(nz, orders[name])
        scratch += [dma((p,)), dma((p,))]
    scratch += [dma((3,)), dma((nt,)), dma((8,))]
    return pl.pallas_call(
        functools.partial(ka_kernel, nf, nt, orders),
        out_shape=[o[0] for o in outs],
        in_specs=[pl.BlockSpec(memory_space=pltpu.SMEM)] + [vm] * 5 + [hb] * 2 + [vm] * 6,
        out_specs=[o[1] for o in outs],
        scratch_shapes=scratch,
        compiler_params=pltpu.CompilerParams(
            collective_id=0, has_side_effects=True, vmem_limit_bytes=56 << 20
        ),
    )(lens, tok, wq, wk, wv, wo, wu, wd, *[v.reshape(1, -1) for v in smalls])


class Scatter:
    def __init__(self, pc, copies, own, land, send, recv, dims, order):
        self.pc, self.copies, self.own, self.land = pc, copies, own, land
        self.send_sem, self.recv_sem, self.dims, self.order = send, recv, dims, order
        self.place = dict(z=pc.z, x=pc.x, y=pc.y, c=pc.c)
        self.stage = 0
        self.count = 0
        self.waits = []

    def index(self, done, at):
        return tuple(at[d] if d in done else slice(None) for d in self.dims)

    def start(self):
        pc, axis = self.pc, self.order[self.stage]
        done = self.order[: self.stage + 1]
        self.waits = []
        for i, step in enumerate(axis_steps(pc, axis)):
            at = dict(self.place)
            at[axis] = lax.rem(pc.z + step["dz"], pc.nz) if axis == "z" else 1 - at[axis]
            dst = self.land[self.stage].at[i]
            n, dev = self.count, pc.rel(**step)
            self.copies.start(self.own.at[self.index(done, at)], dst, self.send_sem.at[n], self.recv_sem.at[n], dev)
            self.waits.append((dst, n, dev))
            self.count += 1

    def arrive(self):
        for dst, n, dev in self.waits:
            wait_recv(dst, self.send_sem.at[n], self.recv_sem.at[n], dev)
        land = self.land[self.stage]
        done = self.order[: self.stage + 1]
        rest = [d for d in self.dims if d not in done]
        sizes = [self.pc.nz if d == "z" else 2 for d in rest]
        count = 1
        for n in sizes:
            count *= n

        def body(i, carry):
            at, k = dict(self.place), i
            for d, n in reversed(list(zip(rest, sizes))):
                at[d] = lax.rem(k, n)
                k = k // n
            dst = self.own.at[tuple(at[d] for d in self.dims)]
            total = dst[...].astype(F32)
            for n in range(len(self.waits)):
                total = total + land[(n,) + tuple(at[d] for d in rest)].astype(F32)
            dst[...] = total.astype(BF)
            return carry

        lax.fori_loop(0, count, body, 0)
        self.stage += 1

    def next(self):
        self.arrive()
        self.start()

    def finish(self, out):
        for dst, n, dev in self.waits:
            wait_recv(dst, self.send_sem.at[n], self.recv_sem.at[n], dev)
        total = self.own[tuple(self.place[d] for d in self.dims)].astype(F32)
        for n in range(len(self.waits)):
            total = total + self.land[self.stage][n].astype(F32)
        out(total)


def landing(nz, dims, order, block):
    out = []
    for k, axis in enumerate(order):
        rest = [d for d in dims if d not in order[: k + 1]]
        n = nz - 1 if axis == "z" else 1
        out.append((n,) + tuple(nz if d == "z" else 2 for d in rest) + block)
    return out


def erf_parts(u):
    half = 0.5 * (1.0 + lax.erf(u * ROOT_HALF))
    return u * half, half + u * jnp.exp2(u * u * (-0.5 * 1.4426950408889634)) * DENSITY


def kc_kernel(
    nf, nt, orders,
    lens, tok, cot, o_own, wo, wqkv, gains, lse, ob, qkv, h1, wu0, wu1, wd0, wd1,
    out_ref, dx_out, gqk_out, gv_out, gwo_out, gwu_out, gwd_out, small_out,
    *rest,
):
    (sm, g1b, g2b, wb, inv2, h2a, dya, fs, hs, hr, dz, dos, dot_all, dop, delta, dhr, dhy, gq0_own, gq1_own, sm_src, sm_dst,
     o_part, u0_own, u1_own, d0_own, d1_own, h2_s, h2_r, dy_s, dy_r, f_s, f_r, hh_s, hh_r, do_s, do_r, dh_s, dh_r,
     st_s, st_r, loc) = rest[:41]
    rest = list(rest[41:])
    lands = {}
    for name in ("o", "u0", "u1", "d0", "d1", "q0", "q1"):
        k = len(orders[name])
        lands[name] = (rest[:k], rest[k], rest[k + 1])
        rest = rest[k + 2 :]
    pc = Place(nf, nt)
    cps = Copies()
    rows, width = tok.shape
    hw = ob.shape[1]
    nh = hw // HD
    groups = rows // 16
    r = width // nf
    c_me, c_other = pc.c, 1 - pc.c
    core = pc.rel(dc=1)

    local = []
    cut = width // 2
    for y in range(2):
        for base, lo, hi in ((y, wu0, wu1), (2 + y, wd0, wd1)):
            local.append((lo.at[y], wb.at[pl.ds(base * width, width), pl.ds(0, cut)]))
            local.append((hi.at[y], wb.at[pl.ds(base * width, width), pl.ds(cut, cut)]))
    weights = []
    for i, (src, dst) in enumerate(local):
        cp = pltpu.make_async_copy(src, dst, loc.at[i])
        cp.start()
        weights.append(cp)
    cot_copy = pltpu.make_async_copy(cot, dya.at[pc.c], loc.at[8])
    cot_copy.start()
    barrier_peers(pc)

    def slot_valid(t, first, count):
        row = iota((count, 1), 0) + (t * rows + first)
        total = lens[0, 0] + lens[0, 1] + lens[0, 2] + lens[0, 3]
        return jnp.where(row < total, 1.0, 0.0)

    half = rows // 2

    def own_dy(j, carry):
        at = pl.ds(pl.multiple_of(j * half, half), half)
        v = slot_valid(pc.t, j * half, half)
        dya[c_me, at, :] = (dya[c_me, at, :].astype(F32) * v).astype(BF)
        return carry

    cot_copy.wait()
    lax.fori_loop(0, 2, own_dy, 0)
    cps.start(dya.at[c_me], dya.at[c_me], dy_s.at[0], dy_r.at[0], core)
    gain, shift = gains[2:3, :], gains[3:4, :]
    none = jnp.zeros((1, width), F32)

    def colsum(x):
        return jnp.sum(x, axis=0, keepdims=True)

    def attn_out(j, carry):
        at = pl.ds(pl.multiple_of(j * half, half), half)
        v = slot_valid(pc.t, j * half, half)
        a = dot_nt(o_own[0, at, :], wo[0])
        for t in range(1, nt):
            a += dot_nt(o_own[t, at, :], wo[t])
        a = a * v
        x = tok[at, :].astype(F32)
        m = x + a
        h, n, inv = layer_norm_rows(m, gain, shift)
        sm[pl.ds(pl.multiple_of(j * half, half), half), :] = m
        sm[pl.ds(pl.multiple_of(rows + j * half, half), half), :] = n
        inv2[at, :] = jnp.broadcast_to(inv, (half, 128))
        h2a[c_me, at, :] = h.astype(BF)
        pltpu.make_async_remote_copy(
            src_ref=h2a.at[c_me, at], dst_ref=h2a.at[c_me, at], send_sem=h2_s.at[j], recv_sem=h2_r.at[j],
            device_id=core, device_id_type=MESH,
        ).start()
        return (carry[0] + colsum(x * x * v), carry[1] + colsum(a * a), carry[2] + colsum(m * m * v))

    sum_x, sum_a, sum_m = lax.fori_loop(0, 2, attn_out, (none, none, none))
    for cp in weights:
        cp.wait()

    def h2_copy(j, slot):
        at = pl.ds(pl.multiple_of(j * half, half), half)
        return pltpu.make_async_remote_copy(
            src_ref=h2a.at[slot, at], dst_ref=h2a.at[slot, at], send_sem=h2_s.at[j], recv_sem=h2_r.at[j],
            device_id=core, device_id_type=MESH,
        )

    def back_copy(j, src, dst, send, recv):
        at = pl.ds(pl.multiple_of(j * half, half), half)
        return pltpu.make_async_remote_copy(
            src_ref=src.at[at], dst_ref=dst.at[at], send_sem=send.at[j], recv_sem=recv.at[j],
            device_id=core, device_id_type=MESH,
        )

    def feed(i, carry):
        far = i // 2
        j = lax.rem(i, 2)
        slot = c_me + far * (1 - 2 * c_me)
        at = pl.ds(pl.multiple_of(j * half, half), half)

        @pl.when(far == 1)
        def _():
            h2_copy(j, c_other).wait_recv()

        @pl.when(i == 2)
        def _():
            wait_recv(dya.at[c_other], dy_s.at[0], dy_r.at[0], core)

        h = h2a[slot, at, :]
        g = dya[slot, at, :]
        f, dh = None, None
        for y in range(2):
            up = wb[y * width : (y + 1) * width, :]
            down = wb[(2 + y) * width : (3 + y) * width, :]
            act, slope = erf_parts(dot_nn(h, up))
            act = act.astype(BF)
            g1b[pl.ds(pl.multiple_of((y * 2 + slot) * rows + j * half, half), half), :] = act
            fy = dot_nt(act, down)
            du = (dot_nn(g, down) * slope).astype(BF)
            g2b[pl.ds((y * 2 + slot) * groups + j * (half // 16), half // 16)] = du.reshape(half // 16, 16, width)
            dy = dot_nt(du, up)
            f = fy if f is None else f + fy
            dh = dy if dh is None else dh + dy

        @pl.when(far == 0)
        def _():
            sm[pl.ds(pl.multiple_of(2 * rows + j * half, half), half), :] = f
            sm[pl.ds(pl.multiple_of(3 * rows + j * half, half), half), :] = dh

        @pl.when(far == 1)
        def _():
            fs[at, :] = f.astype(BF)
            hs[at, :] = dh.astype(BF)
            back_copy(j, hs, hr, hh_s, hh_r).start()
            back_copy(j, fs, fr_in, f_s, f_r).start()

        return carry

    fr_in = hr.at[pl.ds(rows, rows)]
    lax.fori_loop(0, 4, feed, 0)

    def rows_of(ref, y):
        return ref[pl.ds(y * 2 * rows, 2 * rows), :]

    dyall = dya[...].reshape(2 * rows, width)
    part_w = width // 2
    zblk = pc.nz // 2

    def weight_grad(left, get_right, lo, hi):
        for q in range(2):
            lq = left[:, q * part_w : (q + 1) * part_w]

            def body(y, carry, lq=lq, q=q):
                g = dot_tn(lq, get_right(y)).astype(BF)
                lo[y, q * zblk : (q + 1) * zblk] = g[:, :cut].reshape(zblk, 2, r, cut)
                hi[y, q * zblk : (q + 1) * zblk] = g[:, cut:].reshape(zblk, 2, r, cut)
                return carry

            lax.fori_loop(0, 2, body, 0)

    def scatter(name, own, dims):
        land, send, recv = lands[name]
        return Scatter(pc, cps, own, land, send, recv, dims, orders[name])

    weight_grad(dyall, lambda y: g1b[pl.ds(pl.multiple_of(y * 2 * rows, rows), 2 * rows), :], d0_own, d1_own)
    sc_d0 = scatter("d0", d0_own, "yzx")
    sc_d1 = scatter("d1", d1_own, "yzx")
    sc_d0.start()
    sc_d1.start()
    qkv_copy = pltpu.make_async_copy(qkv, g1b, loc.at[0])
    qkv_copy.start()

    def ln_back(j, carry):
        at = pl.ds(pl.multiple_of(j * half, half), half)
        back_copy(j, hs, hr, hh_s, hh_r).wait_recv()
        back_copy(j, fs, fr_in, f_s, f_r).wait_recv()
        v = slot_valid(pc.t, j * half, half)
        e = sm[pl.ds(pl.multiple_of(3 * rows + j * half, half), half), :] + hr[at, :].astype(F32)
        f = sm[pl.ds(pl.multiple_of(2 * rows + j * half, half), half), :]
        f = (f + hr[pl.ds(pl.multiple_of(rows + j * half, half), half), :].astype(F32)) * v
        m = sm[pl.ds(pl.multiple_of(j * half, half), half), :]
        n = sm[pl.ds(pl.multiple_of(rows + j * half, half), half), :]
        out_ref[at, :] = (m + f).astype(BF)
        c = e * gain
        dm = dya[c_me, at, :].astype(F32) + inv2[at, 0:1] * (
            c - jnp.mean(c, axis=-1, keepdims=True) - n * jnp.mean(c * n, axis=-1, keepdims=True)
        )
        dx_out[at, :] = dm
        z = (dm * v).astype(BF)
        dz[at, :] = z
        for t in range(nt):
            d = dot_nn(z, wo[t]).astype(BF)
            dos[t, pl.ds(j * (half // 16), half // 16)] = d.reshape(half // 16, 16, hw)
        return (carry[0] + colsum(e * n), carry[1] + colsum(e), carry[2] + colsum(f * f))

    sum_g2, sum_b2, sum_f = lax.fori_loop(0, 2, ln_back, (none, none, none))
    peers = [pc.rel(dy=1), pc.rel(dy=1, dc=1), core]
    own_groups = pl.ds(pc.t * groups, groups)
    for i, dev in enumerate(peers):
        cps.start(dos.at[dev[1]], dot_all.at[own_groups], do_s.at[i], do_r.at[pc.t], dev)
    cp = pltpu.make_async_copy(dos.at[pc.t], dot_all.at[own_groups], loc.at[2])
    cp.start()
    h1_copy = pltpu.make_async_copy(h1, wb.at[pl.ds(0, nt * rows)], loc.at[1])
    h1_copy.start()

    hall = h2a[...].reshape(2 * rows, width)
    weight_grad(
        hall,
        lambda y: g2b[pl.ds(y * 2 * groups, 2 * groups)].reshape(2 * rows, width),
        u0_own, u1_own,
    )
    sc_u0 = scatter("u0", u0_own, "yzx")
    sc_u1 = scatter("u1", u1_own, "yzx")
    sc_u0.start()
    for t in range(nt):
        o_part[t // 2, t % 2] = dot_tn(dz[...], o_own[t]).astype(BF).reshape(pc.nz, 2, r, hw)
    sc_o = scatter("o", o_part, "yczx")
    sc_o.start()

    small_out[...] = jnp.zeros(small_out.shape, F32)
    tail = 4 * groups
    dot_all[tail:] = jnp.zeros((dot_all.shape[0] - tail, 16, hw), BF)
    sm[...] = jnp.zeros(sm.shape, F32)
    head, mid = MARGIN // 16, (MARGIN + LP) // 16
    g2b[:head] = jnp.zeros((head, 16, width), BF)
    g2b[mid:] = jnp.zeros((g2b.shape[0] - mid, 16, width), BF)
    cp.wait()
    for dev in peers:
        wait_recv(dot_all.at[pl.ds(dev[1] * groups, groups)], do_s.at[0], do_r.at[dev[1]], dev)
    sc_u1.start()
    pack_rows(dot_all, dop, lens, True)

    dlt = LP // 4

    def deltas(j, carry):
        at = pl.ds(pl.multiple_of(j * dlt, 16), dlt)
        prod = dop[at, :].astype(F32) * ob[at, :].astype(F32)
        lane = iota((dlt, 128), 1)
        out = jnp.zeros((dlt, 128), F32)
        for h in range(nh):
            part_h = jnp.where(head_mask(dlt, hw, h), prod, 0.0)
            out = jnp.where(lane == h, jnp.sum(part_h, axis=-1, keepdims=True), out)
        delta[at, :] = out
        return carry

    lax.fori_loop(0, 4, deltas, 0)
    qkv_copy.wait()

    def back(at, keys, h, limit):
        nrow, nkey = at.size, keys.size
        zero = jnp.zeros((), BF)
        hm = head_mask(nrow, hw, h)
        q = jnp.where(hm, g1b[at, :hw], zero)
        s = dot_nt(q, g1b[keys, 256 : 256 + hw])
        p = jnp.exp2(s * EXP_SCALE - lse[at, h : h + 1])
        if limit is not None:
            p = jnp.where(iota(p.shape, 1) < limit, p, 0.0)
        g = jnp.where(hm, dop[at, :], zero)
        dp = dot_nt(g, g1b[keys, 512 : 512 + hw])
        ds = (p * (dp - delta[at, h : h + 1])).astype(BF)
        sm[keys, 512 : 512 + hw] += dot_tn(p.astype(BF), g)
        sm[keys, 256 : 256 + hw] += dot_tn(ds, q)
        km = jnp.where(head_mask(nkey, hw, h), g1b[keys, 256 : 256 + hw], zero)
        sm[at, :hw] += dot_nn(ds, km)

    for h in range(nh):
        def big(j, carry, h=h):
            back(pl.ds(pl.multiple_of(j * 256, 256), 256), pl.ds(0, BIG), h, None)
            return carry

        lax.fori_loop(0, BIG // 256, big, 0)
        def small(k, carry, h=h):
            at = pl.ds(pl.multiple_of(BIG + k * SMALL, 16), SMALL)
            back(at, at, h, small_length(lens, k))
            return carry

        lax.fori_loop(0, 3, small, 0)
        if h == 0:
            sc_d0.next()
            sc_o.next()
        elif h == 1:
            sc_u0.next()
            sc_d1.next()
            sc_o.next()
        else:
            sc_u1.next()
            sc_d0.next()
            sc_o.next()

    seg = segment_matrix(hw)
    gq = own_heads(gains[4:5, :], pc.t, nt, hw)
    gk = own_heads(gains[5:6, :], pc.t, nt, hw)

    def norms(j, carry):
        at = pl.ds(pl.multiple_of(j * dlt, 16), dlt)
        kept = lse[at, :]
        sums, outs = [], []
        for i, g in enumerate((gq, gk)):
            inv = jnp.broadcast_to(kept[:, 8 * (i + 1) : 8 * (i + 1) + 1], (dlt, hw))
            for k in range(1, nh):
                inv = jnp.where(head_mask(dlt, hw, k), kept[:, 8 * (i + 1) + k : 8 * (i + 1) + k + 1], inv)
            n = g1b[at, i * 256 : i * 256 + hw].astype(F32) / g
            e = sm[at, i * 256 : i * 256 + hw] * 0.125
            c = e * g
            d = inv * (c - segment_mean(c, seg) - n * segment_mean(c * n, seg))
            outs.append(d.astype(BF))
            sums.append(colsum(e * n))
        outs.append(sm[at, 512 : 512 + hw].astype(BF))
        for i, d in enumerate(outs):
            g2b[pl.ds(head + j * (dlt // 16), dlt // 16), :, i * 256 : i * 256 + hw] = d.reshape(dlt // 16, 16, hw)
        return (carry[0] + sums[0], carry[1] + sums[1])

    nones = jnp.zeros((1, hw), F32)
    sum_q, sum_k = lax.fori_loop(0, 4, norms, (nones, nones))
    sc_u0.next()
    sc_d1.next()

    def unpack(i, carry):
        out = unpack_tile(g2b, i * 128, lens)
        g1b[pl.ds(pl.multiple_of(i * 128, 128), 128), :] = out.astype(BF)
        return carry

    lax.fori_loop(0, 16, unpack, 0)
    h1_copy.wait()
    sc_u1.next()

    def project(t, sums):
        def body(j, carry):
            at = pl.ds(pl.multiple_of(t * rows + j * half, half), half)
            total = dot_nt(g1b[at, :hw], wqkv[0])
            total += dot_nt(g1b[at, 256 : 256 + hw], wqkv[1])
            total += dot_nt(g1b[at, 512 : 512 + hw], wqkv[2])
            low = total.astype(BF)
            g2b[pl.ds(t * groups + j * (half // 16), half // 16)] = low.reshape(half // 16, 16, width)
            return (carry[0] + colsum(total * wb[at, :].astype(F32)), carry[1] + colsum(total))

        return lax.fori_loop(0, 2, body, sums)

    def add_groups(t, src):
        def body(j, carry):
            at = pl.ds(t * groups + j * 4, 4)
            g2b[at] = (g2b[at].astype(F32) + src[pl.ds(j * 4, 4)].astype(F32)).astype(BF)
            return carry

        lax.fori_loop(0, groups // 4, body, 0)

    def block_of(t):
        return g2b.at[pl.ds(t * groups, groups)]

    t_fo, t_ff = (1 - pc.y) * 2 + c_other, (1 - pc.y) * 2 + c_me
    t_no = pc.y * 2 + c_other
    sc_q = [scatter("q0", gq0_own, "zx"), scatter("q1", gq1_own, "zx")]

    def attn_grad(piece):
        for q in range(2):
            hq = wb[: nt * rows, q * part_w : (q + 1) * part_w]
            if piece == 0:
                g = dot_tn(hq, g1b[: nt * rows, :512])
                g = jnp.concatenate([g[:, :hw], g[:, 256 : 256 + hw]], axis=1)
            else:
                g = dot_tn(hq, g1b[: nt * rows, 512 : 512 + hw])
            own = (gq0_own, gq1_own)[piece]
            own[q * zblk : (q + 1) * zblk] = g.astype(BF).reshape(zblk, 2, r, g.shape[1])
        sc_q[piece].start()

    sums = project(t_fo, (none, none))
    cps.start(block_of(t_fo), dhr.at[0], dh_s.at[0], dh_r.at[0], core)
    sums = project(t_ff, sums)
    wait_recv(dhr.at[0], dh_s.at[0], dh_r.at[0], core)
    add_groups(t_ff, dhr.at[0])
    cps.start(block_of(t_ff), dhy, dh_s.at[2], dh_r.at[2], pc.rel(dy=1))
    attn_grad(0)
    sums = project(t_no, sums)
    cps.start(block_of(t_no), dhr.at[1], dh_s.at[1], dh_r.at[1], core)
    sum_h, sum_d = project(pc.t, sums)
    attn_grad(1)

    gain_one, shift_one = gains[0:1, :], gains[1:2, :]
    small_out[4:5, :hw] = sum_q
    small_out[5:6, :hw] = sum_k
    placed = pltpu.roll(small_out[...], pc.t * hw, 1)
    small_out[...] = placed
    small_out[0:1, :] = (sum_h - shift_one * sum_d) / gain_one
    small_out[1:2, :] = sum_d
    small_out[2:3, :] = sum_g2
    small_out[3:4, :] = sum_b2
    lane = iota((1, width), 1)
    stat = jnp.zeros((1, width), F32)
    counted = jnp.sum(slot_valid(pc.t, 0, rows))
    for i, v in enumerate((sum_x, sum_a, sum_m, sum_f)):
        stat = jnp.where(lane == i, jnp.sum(v), stat)
    small_out[6:7, :] = jnp.where(lane == 4, counted, stat)
    small_stages = [[dict(dc=1)], [dict(dy=1)], [dict(dx=1)], axis_steps(pc, "z")]
    total = small_out[...]

    def small_send(k, total):
        sm_src[k] = total
        for i, step in enumerate(small_stages[k]):
            cps.start(sm_src.at[k], sm_dst.at[k + i], st_s.at[k + i], st_r.at[k + i], pc.rel(**step))

    def small_add(k, total):
        for i, step in enumerate(small_stages[k]):
            wait_recv(sm_dst.at[k + i], st_s.at[k + i], st_r.at[k + i], pc.rel(**step))
            total = total + sm_dst[k + i]
        return total

    small_send(0, total)
    total = small_add(0, total)
    small_send(1, total)
    for s in sc_q:
        s.next()
    total = small_add(1, total)
    small_send(2, total)
    total = small_add(2, total)
    small_send(3, total)

    wait_recv(dhr.at[1], dh_s.at[1], dh_r.at[1], core)
    add_groups(pc.t, dhr.at[1])
    wait_recv(dhy, dh_s.at[2], dh_r.at[2], pc.rel(dy=1))

    def last(j, carry):
        at = pl.ds(pl.multiple_of(j * 128, 128), 128)
        near = g2b[pl.ds(pc.t * groups + j * 8, 8)].astype(F32)
        e = (near + dhy[pl.ds(j * 8, 8)].astype(F32)).reshape(128, width)
        x = tok[at, :].astype(F32)
        _, n, inv = layer_norm_rows(x, gain_one, 0.0)
        c = e * gain_one
        grad = inv * (
            c - jnp.mean(c, axis=-1, keepdims=True) - n * jnp.mean(c * n, axis=-1, keepdims=True)
        )
        dx_out[at, :] = dx_out[at, :] + grad
        return carry

    lax.fori_loop(0, rows // 128, last, 0)
    small_out[...] = small_add(3, total)
    stat = small_out[6:7, :]
    counted = jnp.sum(jnp.where(lane == 4, stat, 0.0))
    small_out[7:8, :] = jnp.where(lane < 4, jnp.sqrt(stat / (counted * width)), 0.0)

    def store(ref, at=None):
        def put(total):
            if at is None:
                ref[...] = total
            else:
                ref[:, at : at + cut] = total

        return put

    sc_q[0].finish(store(gqk_out))
    sc_q[1].finish(store(gv_out))
    sc_o.finish(store(gwo_out))
    sc_d0.finish(store(gwd_out, 0))
    sc_d1.finish(store(gwd_out, cut))
    sc_u0.finish(store(gwu_out, 0))
    sc_u1.finish(store(gwu_out, cut))

    def sent(j, carry):
        h2_copy(j, c_me).wait_send()
        back_copy(j, hs, hr, hh_s, hh_r).wait_send()
        back_copy(j, fs, fr_in, f_s, f_r).wait_send()
        return carry

    lax.fori_loop(0, 2, sent, 0)
    cps.finish()


def call_kc(nf, nt, lens, tok, cot, o_own, wo, wqkv, gains, lse, ob, qkv, h1, wu0, wu1, wd0, wd1):
    nz = nf // 2
    rows, width = tok.shape
    hw = ob.shape[1]
    r = width // nf
    cut = width // 2
    orders = dict(
        o=("c", "x", "y", "z"), u0=("x", "y", "z"), u1=("y", "x", "z"),
        d0=("x", "y", "z"), d1=("z", "x", "y"), q0=("x", "z"), q1=("x", "z"),
    )
    S = jax.ShapeDtypeStruct
    V = pltpu.VMEM
    vm = pl.BlockSpec(memory_space=pltpu.VMEM)
    hb = pl.BlockSpec(memory_space=pl.ANY)
    dma = pltpu.SemaphoreType.DMA
    g3 = (MARGIN + LP + 160) // 16
    outs = [
        S((rows, width), BF), S((rows, width), F32), S((r, 2 * hw), F32), S((r, hw), F32), S((r, hw), F32),
        S((r, width), F32), S((r, width), F32), S((8, width), F32),
    ]
    own = (2, nz, 2, r, cut)
    scratch = [
        V((LP, width), F32), V((LP, width), BF), V((g3, 16, width), BF), V((4 * width, width), BF),
        V((rows, 128), F32), V((2, rows, width), BF), V((2, rows, width), BF),
        V((rows, width), BF), V((rows, width), BF), V((2 * rows, width), BF),
        V((rows, width), BF), V((nt, rows // 16, 16, hw), BF),
        V(((nt * rows + 192) // 16, 16, hw), BF), V((LP, hw), BF), V((LP, 128), F32),
        V((2, rows // 16, 16, width), BF), V((rows // 16, 16, width), BF),
        V((nz, 2, r, 2 * hw), BF), V((nz, 2, r, hw), BF), V((4, 8, width), F32), V((2 + nz, 8, width), F32),
        V((2, 2, nz, 2, r, hw), BF), V(own, BF), V(own, BF), V(own, BF), V(own, BF),
        dma((2,)), dma((2,)), dma((1,)), dma((1,)), dma((2,)), dma((2,)), dma((2,)), dma((2,)),
        dma((3,)), dma((nt,)), dma((3,)), dma((3,)), dma((2 + nz,)), dma((2 + nz,)), dma((9,)),
    ]
    for name in ("o", "u0", "u1", "d0", "d1", "q0", "q1"):
        dims = {"o": "yczx", "q0": "zx", "q1": "zx"}.get(name, "yzx")
        block = (r, {"o": hw, "q0": 2 * hw, "q1": hw}.get(name, cut))
        scratch += [V(shape, BF) for shape in landing(nz, dims, orders[name], block)]
        n = sends_of(nz, orders[name])
        scratch += [dma((n,)), dma((n,))]
    return pl.pallas_call(
        functools.partial(kc_kernel, nf, nt, orders),
        out_shape=outs,
        in_specs=[pl.BlockSpec(memory_space=pltpu.SMEM), vm, hb] + [vm] * 6 + [hb] * 6,
        out_specs=[vm] * 8,
        scratch_shapes=scratch,
        compiler_params=pltpu.CompilerParams(
            collective_id=1, has_side_effects=True, vmem_limit_bytes=64 << 20
        ),
    )(lens, tok, cot, o_own, wo, wqkv, gains, lse, ob, qkv, h1, wu0, wu1, wd0, wd1)


def local_fused(nf, nt, args):
    (tokens, lengths, pictures, w_query, w_key, w_value, w_out, w_up, w_down) = args[:9]
    smalls, cotangent = args[9:15], args[15]
    rows, width = tokens.shape[1:]
    hw = w_query.shape[1]
    per = smalls[0].shape[0]
    place = lax.axis_index("fsdp") * nt + lax.axis_index("tp")
    qkv, lse, ob, wqkv, gains, o_own, h1, wo, *halves = call_ka(
        nf, nt, lengths, tokens[0], w_query, w_key, w_value, w_out, w_up, w_down.T, smalls
    )
    result, grad_in, gqk, gv, gwo, gwu, gwd, small = call_kc(
        nf, nt, lengths, tokens[0], cotangent[0], o_own, wo.reshape(nt, width, hw), wqkv, gains, lse, ob,
        qkv, h1.reshape(nt * rows, width),
        *[w.reshape(2, width, width // 2) for w in halves],
    )
    own = lax.dynamic_slice_in_dim(small, place * per, per, 1)
    statistics = small[7, :4]
    return (
        result[None], grad_in[None],
        gqk[:, :hw], gqk[:, hw:], gv, gwo.T, gwu, gwd.T,
        own[0], own[1], own[2], own[3], own[4], own[5], statistics,
    )


def solution(mesh):
    nf, nt = mesh.shape["fsdp"], mesh.shape["tp"]

    def local(*args):
        tokens, w_query = args[0], args[3]
        if nt == 4 and tokens.shape[0] == 1 and tokens.shape[1] == 512 and w_query.shape[0] % 32 == 0:
            return local_fused(nf, nt, args)
        return local_plain(*args)

    in_specs = (
        P("fsdp", "tp", None),
        P("fsdp", None),
        P("fsdp", None),
        P("fsdp", "tp"),
        P("fsdp", "tp"),
        P("fsdp", "tp"),
        P("tp", "fsdp"),
        P("fsdp", "tp"),
        P("tp", "fsdp"),
        P(("fsdp", "tp")),
        P(("fsdp", "tp")),
        P(("fsdp", "tp")),
        P(("fsdp", "tp")),
        P(("fsdp", "tp")),
        P(("fsdp", "tp")),
        P("fsdp", "tp", None),
    )
    out_specs = (
        P("fsdp", "tp", None),
        P("fsdp", "tp", None),
        P("fsdp", "tp"),
        P("fsdp", "tp"),
        P("fsdp", "tp"),
        P("tp", "fsdp"),
        P("fsdp", "tp"),
        P("tp", "fsdp"),
        P(("fsdp", "tp")),
        P(("fsdp", "tp")),
        P(("fsdp", "tp")),
        P(("fsdp", "tp")),
        P(("fsdp", "tp")),
        P(("fsdp", "tp")),
        P(),
    )
    return jax.shard_map(local, mesh=mesh, in_specs=in_specs, out_specs=out_specs, check_vma=False)
```

profile of v0, /device:TPU:0, one launch (start us, length us, event | category | flops | bytes accessed | tf_op | source)
XLA Modules:
  0.0 215.8 jit_solution(17119088216829386421)
XLA Ops:
  0.7 93.6 %shard_map.262 = (bf16[2368,768]{1,0:T(8,128)(2,1)}, f32[2368,128]{1,0:T(8,128)}, bf16[2368,192]{1,0:T(8,128)(2,1)}, bf16[3,768,192]{2,1,0:T(8,128)(2,1)}, f32[8...) custom-call(s32[1,4]{1,0:T(1,128)} %lens.3, ...), custom_call_target="tpu_custom_call" | custom-call | tf_op jit(solution)/shard_map/pallas_call | solution.py:851
  94.2 110.3 %shard_map.263 = (bf16[512,768]{1,0:T(8,128)(2,1)}, f32[512,768]{1,0:T(8,128)}, f32[96,384]{1,0:T(8,128)}, f32[96,192]{1,0:T(8,128)}, f32[96,192]{1,0:T(8,128)},...) custom-call(s32[1,4]{1,0:T(1,128)} %lens.3, bf16[512,768]{1,0:T(8,128)(2,1)} %bitcast.34, ...), custom_call_target="tpu_custom_call" | custom-call | tf_op jit(solution)/shard_map/pallas_call | solution.py:1452
  204.5 0.0 copy-start
  204.5 1.8 fusion
  206.3 1.6 copy.30
  208.0 0.8 constant_dynamic-slice_fusion
  208.7 0.5 slice_bitcast_fusion.1
  209.3 1.2 slice_bitcast_fusion
  210.5 2.1 copy.36
  212.5 0.0 copy-done
  212.5 0.0 copy-start.3
  212.5 0.0 copy-start.2
  212.5 0.0 copy-start.1
  212.5 1.1 copy.37
  213.7 0.0 copy-done.3
  213.7 0.6 copy.38
  214.3 0.0 copy-done.2
  214.3 0.7 copy.39
  215.0 0.0 copy-done.1
  215.0 0.7 copy.40
Async XLA Ops:
  204.5 8.0 %copy-start = (f32[512,768]{1,0:T(8,128)S(1)}, f32[512,768]{1,0:T(8,128)}, u32[]{:S(2)}) copy-start(f32[512,768]{1,0:T(8,128)} %get-tuple-element.48) | copy-start | bytes 4718596
  212.5 1.2 copy-start.3
  212.5 1.8 copy-start.2
  212.5 2.5 %copy-start.1 = (f32[96,768]{1,0:T(8,128)S(1)}, f32[96,768]{1,0:T(8,128)}, u32[]{:S(2)}) copy-start(f32[96,768]{1,0:T(8,128)} %get-tuple-element.53) | copy-start | bytes 884740
where the time goes:
time: 216 us
  Pallas kernels  204 us (94%)
  local copies, waits for them, and re-layouts  11.2 us (5%)
    pallas_call x1, Pallas kernels, call_kc(): pl.pallas_call(functools.partial(kc_kernel, nf, nt, orders), out_shape=ou...  110 us
    pallas_call x1, Pallas kernels, call_ka(): pl.pallas_call(functools.partial(ka_kernel, nf, nt, orders), out_shape=[o...  93.6 us
    unnamed x14, local copies, waits for them, and re-layouts  6.92 us

commit v1 on v0

--- a/solution.py
+++ b/solution.py
@@ -779,9 +779,6 @@
         if h == 1:
             gu1.wait(1)
             gu1.send(2)
-        elif h == 2:
-            go.wait(2)
-            go.send(3)
 
     ob[...] = of[...].astype(BF)
     for i, (src, dst) in enumerate(((lse, lse_out), (ob, ob_out))):
@@ -802,6 +799,8 @@
         unpack_block(dev[1])
         cps.start(osend.at[dev[1]], o_own.at[pc.t], o_s.at[i], o_r.at[pc.t], dev)
     unpack_block(pc.t)
+    go.wait(2)
+    go.send(3)
     cp = pltpu.make_async_copy(osend.at[pc.t], o_own.at[pc.t], loc.at[1])
     cp.start()
     cp.wait()
@@ -1227,7 +1226,6 @@
         elif h == 1:
             sc_u0.next()
             sc_d1.next()
-            sc_o.next()
         else:
             sc_u1.next()
             sc_d0.next()
@@ -1269,6 +1267,7 @@
     lax.fori_loop(0, 16, unpack, 0)
     h1_copy.wait()
     sc_u1.next()
+    sc_o.next()
 
     def project(t, sums):
         def body(j, carry):
@@ -1394,7 +1393,7 @@
 
     sc_q[0].finish(store(gqk_out))
     sc_q[1].finish(store(gv_out))
-    sc_o.finish(store(gwo_out))
+    sc_o.finish(lambda v: store(gwo_out)(v.T))
     sc_d0.finish(store(gwd_out, 0))
     sc_d1.finish(store(gwd_out, cut))
     sc_u0.finish(store(gwu_out, 0))
@@ -1427,7 +1426,7 @@
     dma = pltpu.SemaphoreType.DMA
     g3 = (MARGIN + LP + 160) // 16
     outs = [
-        S((rows, width), BF), S((rows, width), F32), S((r, 2 * hw), F32), S((r, hw), F32), S((r, hw), F32),
+        S((rows, width), BF), S((rows, width), F32), S((r, 2 * hw), F32), S((r, hw), F32), S((hw, r), F32),
         S((r, width), F32), S((r, width), F32), S((8, width), F32),
     ]
     own = (2, nz, 2, r, cut)
@@ -1480,7 +1479,7 @@
     statistics = small[7, :4]
     return (
         result[None], grad_in[None],
-        gqk[:, :hw], gqk[:, hw:], gv, gwo.T, gwu, gwd.T,
+        gqk[:, :hw], gqk[:, hw:], gv, gwo, gwu, gwd.T,
         own[0], own[1], own[2], own[3], own[4], own[5], statistics,
     )
 

time: 216 us -> 211 us (0.977)
  Pallas kernels: 204 us -> 200 us
    pallas_call x1, Pallas kernels: 110 us -> 108 us  [call_kc(): pl.pallas_call(functools.partial(kc_kernel, nf, nt, orders), out_shape=ou...]
    unnamed x14 -> x16, local copies, waits for them, and re-layouts: 6.92 us -> 5.94 us
where the time goes in v1:
time: 211 us
  Pallas kernels  200 us (95%)
  local copies, waits for them, and re-layouts  10.2 us (5%)
    pallas_call x1, Pallas kernels, call_kc(): pl.pallas_call(functools.partial(kc_kernel, nf, nt, orders), out_shape=ou...  108 us
    pallas_call x1, Pallas kernels, call_ka(): pl.pallas_call(functools.partial(ka_kernel, nf, nt, orders), out_shape=[o...  92 us
    unnamed x16, local copies, waits for them, and re-layouts  5.94 us

profile of v1, /device:TPU:0, one launch (start us, length us, event | category | flops | bytes accessed | tf_op | source)
XLA Modules:
  0.0 211.0 jit_solution(5884114413219987080)
XLA Ops:
  0.7 92.0 %shard_map.262 = (bf16[2368,768]{1,0:T(8,128)(2,1)}, f32[2368,128]{1,0:T(8,128)}, bf16[2368,192]{1,0:T(8,128)(2,1)}, bf16[3,768,192]{2,1,0:T(8,128)(2,1)}, f32[8...) custom-call(s32[1,4]{1,0:T(1,128)} %lens.3, ...), custom_call_target="tpu_custom_call" | custom-call | tf_op jit(solution)/shard_map/pallas_call | solution.py:850
  92.7 108.1 %shard_map.263 = (bf16[512,768]{1,0:T(8,128)(2,1)}, f32[512,768]{1,0:T(8,128)}, f32[96,384]{1,0:T(8,128)}, f32[96,192]{1,0:T(8,128)}, f32[192,96]{1,0:T(8,128)},...) custom-call(s32[1,4]{1,0:T(1,128)} %lens.3, bf16[512,768]{1,0:T(8,128)(2,1)} %bitcast.33, ...), custom_call_target="tpu_custom_call" | custom-call | tf_op jit(solution)/shard_map/pallas_call | solution.py:1451
  200.8 0.0 copy-start
  200.8 1.8 fusion
  202.6 0.8 constant_dynamic-slice_fusion
  203.4 0.5 slice_bitcast_fusion.1
  203.9 1.2 slice_bitcast_fusion
  205.1 2.1 copy.36
  207.1 0.0 copy-done
  207.1 0.0 copy-start.4
  207.2 0.0 copy-start.3
  207.2 0.0 copy-start.2
  207.2 0.0 copy-start.1
  207.2 1.1 copy.37
  208.3 0.0 copy-done.4
  208.3 0.6 copy.38
  209.0 0.0 copy-done.3
  209.0 0.6 copy.39
  209.6 0.0 copy-done.2
  209.6 0.7 copy.40
  210.3 0.0 copy-done.1
  210.3 0.7 copy.41
Async XLA Ops:
  200.8 6.4 %copy-start = (f32[512,768]{1,0:T(8,128)S(1)}, f32[512,768]{1,0:T(8,128)}, u32[]{:S(2)}) copy-start(f32[512,768]{1,0:T(8,128)} %get-tuple-element.48) | copy-start | bytes 4718596
  207.1 1.2 copy-start.4
  207.2 1.8 copy-start.3
  207.2 2.5 %copy-start.2 = (f32[96,768]{1,0:T(8,128)S(1)}, f32[96,768]{1,0:T(8,128)}, u32[]{:S(2)}) copy-start(f32[96,768]{1,0:T(8,128)} %get-tuple-element.84) | copy-start | bytes 884740
  207.2 3.2 %copy-start.1 = (f32[96,768]{1,0:T(8,128)S(1)}, f32[96,768]{1,0:T(8,128)}, u32[]{:S(2)}) copy-start(f32[96,768]{1,0:T(8,128)} %get-tuple-element.53) | copy-start | bytes 884740
